TPU v7x, 256 devices: a whole 4x4x8 slice. The times are simulated.
256 devices in a mesh: trav: 8 (over z), bulk: 32 (over y, x, core).
Axes of the slice: x: 4, y: 4, z: 8, core: 2. Of those that a mesh axis runs over, the one named last changes fastest.
Arguments:
- parents: bfloat16 [49152, 1024], P(('trav', 'bulk')), may hold values from -6 to 6
- act_table: bfloat16 [128, 1024], replicated, may hold values from -5 to 5
- bucket_table: bfloat16 [8192, 1024], P('bulk'), may hold values from -5 to 5
- w_first: bfloat16 [1024, 2048], P(('trav', 'bulk')), may hold values from -0.1875 to 0.1875
- b_first: float32 [2048], replicated, may hold values from -3 to 3
- w_second: bfloat16 [2048, 2048], P(('trav', 'bulk')), may hold values from -0.1875 to 0.1875
- b_second: float32 [2048], replicated, may hold values from -3 to 3
- w_head: bfloat16 [2048, 8], replicated, may hold values from -0.1875 to 0.1875
- b_head: float32 [8], replicated, may hold values from -3 to 3
- branch_counts: int32 [49152], P(('trav', 'bulk')), may hold values from 1 to 4
- sampled_actions: int32 [49152, 4], P(('trav', 'bulk')), may hold values from 0 to 127
- bucket_owner: int32 [49152, 1], P(('trav', 'bulk')), may hold values from 0 to 31; in each aligned block of 192 rows (0 to 191, 192 to 383, ...) at most 8 rows name the same one
- bucket_row: int32 [49152], P(('trav', 'bulk')), may hold values from 0 to 255
- legal_mask: int32 [49152, 32], P(('trav', 'bulk')), may hold values 0 or 1
- ancestor: int32 [49152], P(('trav', 'bulk')), may hold values from 0 to 47
Outputs:
- strategy: float32 [49152, 32], P(('trav', 'bulk'))
- ancestor_value: float32 [12288], P(('trav', 'bulk'))
Inputs may be any that keep to these rules, and one draw needn't show every extreme that they name: `bucket_owner`: in each aligned block of 192 histories (the histories of one device) no evaluator is named more than 8 times, a bound that some block reaches.
All inputs are finite; a program needn't handle non-finite values. No bound on the sum of `legal_mask` on one device may be relied on, other than what follows from the above.
Results may differ from a plain program's by a relative error of at most 0.0078.
Values may be sent and summed in bfloat16 or wider, within the bound.
A program may use at most 64 MiB of HBM per device.

v0:
```python
import jax
import jax.numpy as jnp
from jax import lax
from jax.sharding import PartitionSpec as P

tremble = 0.05


def network(inputs, w_first, b_first, w_second, b_second, w_head, b_head):
    columns = inputs
    first = jnp.dot(
        columns,
        lax.all_gather(w_first, ("trav", "bulk"), axis=0, tiled=True),
        preferred_element_type=jnp.float32,
    )
    hidden_one = jnp.maximum(first + b_first, 0.0).astype(jnp.bfloat16)
    columns = hidden_one
    second = jnp.dot(
        columns,
        lax.all_gather(w_second, ("trav", "bulk"), axis=0, tiled=True),
        preferred_element_type=jnp.float32,
    )
    hidden_two = jnp.maximum(second + b_second, 0.0).astype(jnp.bfloat16)
    return jnp.dot(hidden_two, w_head, preferred_element_type=jnp.float32) + b_head


def body(
    parents,
    act_table,
    bucket_table,
    w_first,
    b_first,
    w_second,
    b_second,
    w_head,
    b_head,
    branch_counts,
    sampled_actions,
    bucket_owner,
    bucket_row,
    legal_mask,
    ancestor,
):
    par_count = parents.shape[0]
    feature_count = parents.shape[1]
    branch_slots = sampled_actions.shape[1]
    vocab_size = act_table.shape[0]
    action_count = w_head.shape[1]
    bulk_count = lax.axis_size("bulk")
    capacity = max(2, (4 * par_count + 3 * bulk_count - 1) // (3 * bulk_count))
    slot_total = bulk_count * capacity
    action_onehot = (
        sampled_actions.reshape(-1)[:, None] == jnp.arange(vocab_size)[None, :]
    ).astype(jnp.bfloat16)
    act_rows = jnp.dot(action_onehot, act_table, preferred_element_type=jnp.float32)
    base = (jnp.repeat(parents.astype(jnp.float32), branch_slots, axis=0) + act_rows).astype(
        jnp.bfloat16
    )
    base = lax.optimization_barrier(base)
    owner_index = bucket_owner[:, 0]
    owner_hits = (owner_index[:, None] == jnp.arange(bulk_count)[None, :]).astype(jnp.int32)
    earlier = jnp.cumsum(owner_hits, axis=0) - owner_hits
    slot_index = owner_index * capacity + jnp.sum(earlier * owner_hits, axis=1)
    placement_int = (slot_index[None, :] == jnp.arange(slot_total)[:, None]).astype(jnp.int32)
    slot_bucket = jnp.sum(placement_int * bucket_row[None, :], axis=1).reshape(bulk_count, capacity)
    placement = placement_int.astype(jnp.bfloat16)
    outgoing = jnp.dot(
        placement,
        base.reshape(par_count, branch_slots * feature_count),
        preferred_element_type=jnp.float32,
    )
    outgoing = outgoing.astype(jnp.bfloat16).reshape(
        bulk_count, capacity * branch_slots, feature_count
    )
    arrived_rows = lax.all_to_all(outgoing, "bulk", split_axis=0, concat_axis=0, tiled=True)
    arrived_ids = lax.all_to_all(slot_bucket, "bulk", split_axis=0, concat_axis=0, tiled=True)
    table_rows = jnp.take(bucket_table, arrived_ids.reshape(-1), axis=0)
    inputs = (
        arrived_rows.reshape(slot_total, branch_slots, feature_count).astype(jnp.float32)
        + table_rows.astype(jnp.float32)[:, None, :]
    )
    inputs = inputs.astype(jnp.bfloat16).reshape(slot_total * branch_slots, feature_count)
    evaluated = network(inputs, w_first, b_first, w_second, b_second, w_head, b_head)
    returned = lax.all_to_all(
        evaluated.reshape(bulk_count, capacity * branch_slots * action_count).astype(jnp.bfloat16),
        "bulk",
        split_axis=0,
        concat_axis=0,
        tiled=True,
    ).astype(jnp.float32)
    advantage = jnp.take(
        returned.reshape(slot_total, branch_slots * action_count), slot_index, axis=0
    )
    advantage = advantage.reshape(par_count, branch_slots, action_count)
    first_action = (jnp.arange(action_count) == 0).astype(jnp.float32)
    allowed = jnp.maximum(
        legal_mask.reshape(par_count, branch_slots, action_count).astype(jnp.float32), first_action
    )
    positive = allowed * (jnp.maximum(advantage, 0.0) + tremble)
    sigma = positive / jnp.sum(positive, axis=-1, keepdims=True)
    live = (jnp.arange(branch_slots)[None, :] < branch_counts[:, None]).astype(jnp.float32)
    strategy = (sigma * live[:, :, None]).reshape(par_count, branch_slots * action_count)
    branch_value = jnp.sum(sigma * advantage, axis=-1)
    history_value = jnp.sum(branch_value * live, axis=1) / branch_counts.astype(jnp.float32)
    node_count = par_count // 4
    node_onehot = (ancestor[:, None] == jnp.arange(node_count)[None, :]).astype(jnp.float32)
    ancestor_value = jnp.sum(node_onehot * history_value[:, None], axis=0)
    return (strategy, ancestor_value)


def solution(mesh):
    return jax.shard_map(
        body,
        mesh=mesh,
        in_specs=(
            P(("trav", "bulk"), None),
            P(),
            P("bulk", None),
            P(("trav", "bulk"), None),
            P(),
            P(("trav", "bulk"), None),
            P(),
            P(),
            P(),
            P(("trav", "bulk")),
            P(("trav", "bulk"), None),
            P(("trav", "bulk"), None),
            P(("trav", "bulk")),
            P(("trav", "bulk"), None),
            P(("trav", "bulk")),
        ),
        out_specs=(P(("trav", "bulk"), None), P(("trav", "bulk"))),
        check_vma=False,
    )
```

profile of v0, /device:TPU:1, one launch (start us, length us, event | category | flops | bytes accessed | tf_op | source)
XLA Modules:
  0.0 301.7 jit_solution(12102274634874806539)
XLA Ops:
  8.0 0.7 all-gather.4.cloned.1.call-update
  10.3 0.7 fusion.12
  11.7 0.8 select_reduce_fusion
  12.5 0.7 all_to_all.14
  13.2 8.6 %all-to-all-start.1 = ((s32[32,1,8]{2,1,0:T(1,128)}), s32[32,1,8]{2,1,0:T(1,128)S(1)}, u32[]{:S(2)}, u32[]{:S(2)}) async-start(s32[32,1,8]{2,1,0:T(1,128)} %bitcast.4), calls=%async_computation.1 | async-start | bytes 32768 | tf_op jit(solution)/shard_map/all_to_all | solution.py:76
  21.8 3.5 %broadcast_in_dim.48 = f32[192,4,1024]{2,1,0:T(4,128)} broadcast(bf16[192,1024]{1,0:T(8,128)(2,1)} %param.15), dimensions={0,2} | broadcast | bytes 3538944 | tf_op jit(solution)/shard_map/broadcast_in_dim | solution.py:56
  25.3 5.0 %reshape.171 = f32[768,1024]{1,0:T(8,128)} reshape(f32[192,4,1024]{2,1,0:T(4,128)} %broadcast_in_dim.48) | data formatting | bytes 6291456 | tf_op jit(solution)/shard_map/reshape | solution.py:56
  30.6 2.5 add_convert_fusion
  33.1 2.3 reshape.172
  35.3 2.2 convolution_convert_fusion
  37.6 2.6 reshape.173
  40.2 7.4 %all-to-all-start = ((bf16[32,32,1024]{2,1,0:T(8,128)(2,1)}), bf16[32,32,1024]{2,1,0:T(8,128)(2,1)S(1)}, u32[]{:S(2)}, u32[]{:S(2)}) async-start(bf16[32,32,1024]{2,1,0:T(8,128)(2,1)} %reshape.173), calls=%async_computation | async-start | bytes 4194304 | tf_op jit(solution)/shard_map/all_to_all | solution.py:75
  49.1 1.2 gather_fusion
  50.4 3.1 %add.100 = f32[256,4,1024]{2,1,0:T(4,128)} broadcast(f32[256,1024]{1,0:T(8,128)S(1)} %select_convert_fusion), dimensions={0,2} | broadcast | bytes 5242880 | tf_op jit(solution)/shard_map/add | solution.py:79
  53.5 5.3 %add.101 = f32[1024,1024]{1,0:T(8,128)} reshape(f32[256,4,1024]{2,1,0:T(4,128)} %add.100) | data formatting | bytes 8388608 | tf_op jit(solution)/shard_map/add | solution.py:79
  58.8 76.4 %all-gather.6.cloned.1.call-done = bf16[256,4,2048]{2,1,0:T(4,128)(2,1)} async-done(((bf16[1,4,2048]{2,1,0:T(4,128)(2,1)}), bf16[256,4,2048]{2,1,0:T(4,128)(2,1)}) %all-gather.6.cloned.1.call-update) | async-done | bytes 4194320 | tf_op jit(solution)/shard_map/all_gather | solution.py:13
  135.3 6.9 %reshape.196 = bf16[1024,2048]{1,0:T(8,128)(2,1)} reshape(bf16[256,4,2048]{2,1,0:T(4,128)(2,1)} %all-gather.6.cloned.1.call-done) | data formatting | bytes 8388608
  142.2 111.8 %all-gather.4.cloned.1.call-done = bf16[2048,2048]{1,0:T(8,128)(2,1)} async-done(((bf16[8,2048]{1,0:T(8,128)(2,1)}), bf16[2048,2048]{1,0:T(8,128)(2,1)}) %all-gather.4.cloned.1.call-update) | async-done | bytes 8388624 | tf_op jit(solution)/shard_map/all_gather | solution.py:20
  254.1 19.9 %maximum_convert_fusion = bf16[1024,2048]{1,0:T(8,128)(2,1)} fusion(bf16[2048,2048]{1,0:T(8,128)(2,1)} %all-gather.4.cloned.1.call-done, bf16[1024,2048]{1,0:T(8,128)(2,1)} %reshape.196, f32[2048]{0:T(1024)S(1)} %copy-done.9, f32[2048]{0:T(1024)S(1)} %copy-done.10, f32[1024,1024]{1,0:T(8,128)} %add.101, bf16[1024,1024]{1,0:T(8,128)(2,1)S(1)} %bitcast.51), kind=kOutput, calls=%fused_computation.2 | convolution fusion | flops 12900630528 | bytes 23085056 | tf_op jit(solution)/shard_map/dot_general | solution.py:18
  274.0 3.4 %fusion.8 = bf16[1024,8]{0,1:T(8,128)(2,1)S(1)} fusion(bf16[1024,2048]{1,0:T(8,128)(2,1)} %maximum_convert_fusion, bf16[2048,8]{0,1:T(8,128)(2,1)S(1)} %copy-done.3, f32[8]{0:T(128)S(1)} %copy-done.7), kind=kOutput, calls=%fused_computation.13 | convolution fusion | flops 33570816 | bytes 4243488 | tf_op jit(solution)/shard_map/dot_general | solution.py:24
  278.3 0.7 reduce.12
  279.7 5.8 %all-to-all-start.2 = ((bf16[32,2,128]{2,1,0:T(2,128)(2,1)}), bf16[32,2,128]{2,1,0:T(2,128)(2,1)S(1)}, u32[]{:S(2)}, u32[]{:S(2)}) async-start(bf16[32,2,128]{2,1,0:T(2,128)(2,1)} %reshape.212), calls=%async_computation.2 | async-start | bytes 32768 | tf_op jit(solution)/shard_map/all_to_all | solution.py:84
  285.6 6.8 %all-to-all-done.2 = bf16[32,2,128]{2,1,0:T(2,128)(2,1)S(1)} async-done(((bf16[32,2,128]{2,1,0:T(2,128)(2,1)}), bf16[32,2,128]{2,1,0:T(2,128)(2,1)S(1)}, u32[]{:S(2)}, u32[]{:S(2)}) %all-to-all-start.2) | async-done | bytes 16416 | tf_op jit(solution)/shard_map/all_to_all | solution.py:84
  292.6 0.7 gather_fusion.1
  (65 shorter events, 8.3 us)
Async XLA Ops:
  7.2 41.9 %copy-start = (bf16[256,1024]{1,0:T(8,128)(2,1)S(1)}, bf16[256,1024]{1,0:T(8,128)(2,1)}, u32[]{:S(2)}) copy-start(bf16[256,1024]{1,0:T(8,128)(2,1)} %param.17) | copy-start | bytes 1572868
  7.2 128.1 %all-gather.6.cloned.1.call-start = ((), (), s32[]{:S(2)}) async-start(), calls=%async_computation.4 | async-start | bytes 4210688 | tf_op jit(solution)/shard_map/all_gather | solution.py:13
  7.9 246.1 %all-gather.4.cloned.1.call-start = ((), (), s32[]{:S(2)}) async-start(), calls=%async_computation.3 | async-start | bytes 8421376 | tf_op jit(solution)/shard_map/all_gather | solution.py:20
  13.2 27.0 %all-to-all-start.1 = ((s32[32,1,8]{2,1,0:T(1,128)}), s32[32,1,8]{2,1,0:T(1,128)S(1)}, u32[]{:S(2)}, u32[]{:S(2)}) async-start(s32[32,1,8]{2,1,0:T(1,128)} %bitcast.4), calls=%async_computation.1 | async-start | bytes 32768 | tf_op jit(solution)/shard_map/all_to_all | solution.py:76
  21.8 8.5 %copy-start.6 = (s32[192,4]{0,1:T(4,128)S(1)}, s32[192,4]{0,1:T(4,128)}, u32[]{:S(2)}) copy-start(s32[192,4]{0,1:T(4,128)} %param.25) | copy-start | bytes 9220
  21.8 8.8 %copy-start.2 = (bf16[128,1024]{1,0:T(8,128)(2,1)S(1)}, bf16[128,1024]{1,0:T(8,128)(2,1)}, u32[]{:S(2)}) copy-start(bf16[128,1024]{1,0:T(8,128)(2,1)} %param.16) | copy-start | bytes 786436
  37.5 10.0 %copy-start.4 = (s32[192,1]{0,1:T(1,128)S(1)}, s32[192,1]{0,1:T(1,128)}, u32[]{:S(2)}) copy-start(s32[192,1]{0,1:T(1,128)} %param.26) | copy-start | bytes 2308
  37.6 10.1 %copy-start.5 = (s32[192]{0:T(256)S(1)}, s32[192]{0:T(256)}, u32[]{:S(2)}) copy-start(s32[192]{0:T(256)} %param.24) | copy-start | bytes 2308
  40.2 102.0 %all-to-all-start = ((bf16[32,32,1024]{2,1,0:T(8,128)(2,1)}), bf16[32,32,1024]{2,1,0:T(8,128)(2,1)S(1)}, u32[]{:S(2)}, u32[]{:S(2)}) async-start(bf16[32,32,1024]{2,1,0:T(8,128)(2,1)} %reshape.173), calls=%async_computation | async-start | bytes 4194304 | tf_op jit(solution)/shard_map/all_to_all | solution.py:75
  58.8 195.2 %copy-start.9 = (f32[2048]{0:T(1024)S(1)}, f32[2048]{0:T(1024)}, u32[]{:S(2)}) copy-start(f32[2048]{0:T(1024)} %param.21) | copy-start | bytes 24580
  58.8 195.2 %copy-start.10 = (f32[2048]{0:T(1024)S(1)}, f32[2048]{0:T(1024)}, u32[]{:S(2)}) copy-start(f32[2048]{0:T(1024)} %param.19) | copy-start | bytes 24580
  254.1 19.9 %copy-start.3 = (bf16[2048,8]{0,1:T(8,128)(2,1)S(1)}, bf16[2048,8]{0,1:T(8,128)(2,1)}, u32[]{:S(2)}) copy-start(bf16[2048,8]{0,1:T(8,128)(2,1)} %param.22) | copy-start | bytes 98308
  254.1 19.9 %copy-start.7 = (f32[8]{0:T(128)S(1)}, f32[8]{0:T(128)}, u32[]{:S(2)}) copy-start(f32[8]{0:T(128)} %param.23) | copy-start | bytes 100
  274.0 19.3 %copy-start.1 = (s32[192,32]{0,1:T(8,128)S(1)}, s32[192,32]{0,1:T(8,128)}, u32[]{:S(2)}) copy-start(s32[192,32]{0,1:T(8,128)} %param.28) | copy-start | bytes 73732
  274.0 19.6 %copy-start.8 = (s32[192]{0:T(256)S(1)}, s32[192]{0:T(256)}, u32[]{:S(2)}) copy-start(s32[192]{0:T(256)} %param.29) | copy-start | bytes 2308
  279.7 12.7 %all-to-all-start.2 = ((bf16[32,2,128]{2,1,0:T(2,128)(2,1)}), bf16[32,2,128]{2,1,0:T(2,128)(2,1)S(1)}, u32[]{:S(2)}, u32[]{:S(2)}) async-start(bf16[32,2,128]{2,1,0:T(2,128)(2,1)} %reshape.212), calls=%async_computation.2 | async-start | bytes 32768 | tf_op jit(solution)/shard_map/all_to_all | solution.py:84
Sparse Core Ops, SparseCore 0:
  11.6 123.6 all-gather.5
  138.9 115.1 all-gather.3
where the time goes:
time: 302 us
  waiting for transfers between devices  196 us (65%)
  local copies, waits for them, and re-layouts  34.3 us (11%)
  matrix products  28 us (9%)
  starting transfers between devices  21.8 us (7%)
  between operations  14.3 us (5%)
  other arithmetic  6.85 us (2%)
    all_gather x1, waiting for transfers between devices, network(): lax.all_gather(w_second, ('trav', 'bulk'), axis=0, tiled=True)  112 us
    all_gather x1, waiting for transfers between devices, network(): lax.all_gather(w_first, ('trav', 'bulk'), axis=0, tiled=True)  76.4 us
    dot_general x1, matrix products, network(): jnp.dot(columns, lax.all_gather(w_second, ('trav', 'bulk'), axis=0, tiled...  19.9 us
    all_to_all x1, starting transfers between devices, body(): lax.all_to_all(slot_bucket, 'bulk', split_axis=0, concat_axis=0, tiled=True)  8.58 us
    add x2, local copies, waits for them, and re-layouts, body(): arrived_rows.reshape(slot_total, branch_slots, feature_count)  8.44 us
    unnamed x26, local copies, waits for them, and re-layouts  7.71 us
    all_to_all x1, starting transfers between devices, body(): lax.all_to_all(outgoing, 'bulk', split_axis=0, concat_axis=0, tiled=True)  7.38 us
    all_to_all x1, waiting for transfers between devices, body(): lax.all_to_all(evaluated.reshape(bulk_count, capacity * branch_slots * ac...  6.79 us
  transfers between devices with their start and end apart: 5, of which 3 were waited for; matrix products, arithmetic and copies ran while one was open for 13% of the time, Pallas kernels for 0%

commit v1 on v0

--- a/solution.py
+++ b/solution.py
@@ -10,7 +10,12 @@
     columns = inputs
     first = jnp.dot(
         columns,
-        lax.all_gather(w_first, ("trav", "bulk"), axis=0, tiled=True),
+        jnp.concatenate(
+            lax.all_to_all(
+                jnp.stack([w_first] * lax.axis_size(("trav", "bulk"))), ("trav", "bulk"), 0, 0
+            ),
+            axis=0,
+        ),
         preferred_element_type=jnp.float32,
     )
     hidden_one = jnp.maximum(first + b_first, 0.0).astype(jnp.bfloat16)

time: 302 us -> 258 us (0.85)
  waiting for transfers between devices: 196 us -> 105 us
  blocking collectives: 0 us -> 36.7 us
  starting transfers between devices: 21.8 us -> 27.4 us
  other arithmetic: 6.85 us -> 11.5 us
    all_gather x1, waiting for transfers between devices: 112 us -> 0.01 us  [network(): lax.all_gather(w_second, ('trav', 'bulk'), axis=0, tiled=True)]
    all_to_all x1, waiting for transfers between devices: 0.01 us -> 97.1 us  [network(): lax.all_to_all(jnp.stack([w_first] * lax.axis_size(('trav', 'bulk'))), ('...]
    all_gather x1 -> x0, waiting for transfers between devices: 76.4 us -> none  [network(): lax.all_gather(w_first, ('trav', 'bulk'), axis=0, tiled=True)]
    all_to_all x0 -> x1, blocking collectives: none -> 36.7 us  [body(): lax.all_to_all(outgoing, 'bulk', split_axis=0, concat_axis=0, tiled=True)]
    add x2 -> x0, local copies, waits for them, and re-layouts: 8.44 us -> none  [body(): arrived_rows.reshape(slot_total, branch_slots, feature_count)]
    unnamed x26 -> x29, local copies, waits for them, and re-layouts: 7.71 us -> 0.81 us
    reshape x0 -> x1, local copies, waits for them, and re-layouts: none -> 6.89 us  [network(): jnp.concatenate(lax.all_to_all(jnp.stack([w_first] * lax.axis_size(('trav...]
    all_to_all x1, starting transfers between devices: 7.38 us -> 12.7 us  [network(): lax.all_to_all(jnp.stack([w_first] * lax.axis_size(('trav', 'bulk'))), ('...]
  transfers between devices with their start and end apart: 5 -> 4, of which waited for: 3 -> 2; matrix products, arithmetic and copies ran while one was open for 13% -> 18% of each run, Pallas kernels for 0% -> 0%
where the time goes in v1:
time: 258 us; the launch traced here: 257 us
  waiting for transfers between devices  105 us (41%)
  blocking collectives  36.7 us (14%)
  local copies, waits for them, and re-layouts  35.1 us (14%)
  matrix products  27.9 us (11%)
  starting transfers between devices  27.4 us (11%)
  between operations  14.3 us (6%)
  other arithmetic  11.5 us (4%)
    all_to_all x1, waiting for transfers between devices, network(): lax.all_to_all(jnp.stack([w_first] * lax.axis_size(('trav', 'bulk'))), ('...  97.1 us
    all_to_all x1, blocking collectives, body(): lax.all_to_all(outgoing, 'bulk', split_axis=0, concat_axis=0, tiled=True)  36.7 us
    dot_general x1, matrix products, network(): jnp.dot(columns, lax.all_gather(w_second, ('trav', 'bulk'), axis=0, tiled...  19.8 us
    all_to_all x1, starting transfers between devices, network(): lax.all_to_all(jnp.stack([w_first] * lax.axis_size(('trav', 'bulk'))), ('...  12.7 us
    all_to_all x1, starting transfers between devices, body(): lax.all_to_all(slot_bucket, 'bulk', split_axis=0, concat_axis=0, tiled=True)  8.58 us
    reshape x1, local copies, waits for them, and re-layouts, network(): jnp.concatenate(lax.all_to_all(jnp.stack([w_first] * lax.axis_size(('trav...  6.89 us
    all_to_all x1, waiting for transfers between devices, body(): lax.all_to_all(evaluated.reshape(bulk_count, capacity * branch_slots * ac...  6.79 us
    all_to_all x1, starting transfers between devices, body(): lax.all_to_all(evaluated.reshape(bulk_count, capacity * branch_slots * ac...  6.03 us
  transfers between devices with their start and end apart: 4, of which 2 were waited for; matrix products, arithmetic and copies ran while one was open for 18% of the time, Pallas kernels for 0%

profile of v1, /device:TPU:1, one launch (start us, length us, event | category | flops | bytes accessed | tf_op | source)
XLA Modules:
  0.0 257.4 jit_solution(684643269900110543)
XLA Ops:
  9.5 0.7 fusion.9
  10.9 0.8 select_reduce_fusion
  12.4 8.6 %all-to-all-start.1 = ((s32[32,1,8]{2,1,0:T(1,128)}), s32[32,1,8]{2,1,0:T(1,128)S(1)}, u32[]{:S(2)}, u32[]{:S(2)}) async-start(s32[32,1,8]{2,1,0:T(1,128)} %bitcast.3), calls=%async_computation.1 | async-start | bytes 32768 | tf_op jit(solution)/shard_map/all_to_all | solution.py:81
  21.0 3.6 %broadcast_in_dim.48 = f32[192,4,1024]{2,1,0:T(4,128)} broadcast(bf16[192,1024]{1,0:T(8,128)(2,1)} %param.15), dimensions={0,2} | broadcast | bytes 3538944 | tf_op jit(solution)/shard_map/broadcast_in_dim | solution.py:61
  24.7 4.9 %reshape.190 = f32[768,1024]{1,0:T(8,128)} reshape(f32[192,4,1024]{2,1,0:T(4,128)} %broadcast_in_dim.48) | data formatting | bytes 6291456 | tf_op jit(solution)/shard_map/reshape | solution.py:61
  29.8 2.5 add_convert_fusion.1
  32.3 2.3 reshape.191
  34.6 2.2 convolution_convert_fusion
  36.9 2.6 %reshape.192 = bf16[32,32,1024]{2,1,0:T(8,128)(2,1)} reshape(bf16[256,4096]{1,0:T(8,128)(2,1)S(1)} %convolution_convert_fusion) | data formatting | bytes 4194304 | tf_op jit(solution)/shard_map/reshape | solution.py:77
  39.5 36.7 %all_to_all.25 = bf16[32,32,1024]{2,1,0:T(8,128)(2,1)S(1)} all-to-all(bf16[32,32,1024]{2,1,0:T(8,128)(2,1)} %reshape.192), channel_id=1, replica_groups=mesh['trav'=8,'bulk'=32] {'bulk'}, dimensions={0} | all-to-all | bytes 4194304 | tf_op jit(solution)/shard_map/all_to_all | solution.py:80
  76.2 4.1 %stack.2 = bf16[256,4,2048]{2,1,0:T(4,128)(2,1)} broadcast(bf16[4,2048]{1,0:T(4,128)(2,1)S(1)} %copy-done.5), dimensions={1,2} | broadcast | bytes 4210688 | tf_op jit(solution)/shard_map/stack | solution.py:15
  80.3 12.7 %all-to-all-start.2 = ((bf16[256,4,2048]{2,1,0:T(4,128)(2,1)}), bf16[256,4,2048]{2,1,0:T(4,128)(2,1)}, u32[]{:S(2)}, u32[]{:S(2)}) async-start(bf16[256,4,2048]{2,1,0:T(4,128)(2,1)} %stack.2), calls=%async_computation.2 | async-start | bytes 8388608 | tf_op jit(solution)/shard_map/all_to_all | solution.py:14
  94.5 1.2 gather_fusion
  95.6 1.1 select_convert_fusion
  96.8 3.0 %reshape.197 = f32[256,4,1024]{2,1,0:T(4,128)} reshape(bf16[32,32,1024]{2,1,0:T(8,128)(2,1)S(1)} %all_to_all.25) | data formatting | bytes 6291456 | tf_op jit(solution)/shard_map/convert_element_type | solution.py:84
  99.8 3.7 %add_convert_fusion = bf16[256,4,1024]{2,1,0:T(4,128)(2,1)S(1)} fusion(f32[256,4,1024]{2,1,0:T(4,128)} %reshape.197, f32[256,1024]{1,0:T(8,128)} %select_convert_fusion), kind=kLoop, calls=%fused_computation.9 | loop fusion | flops 2097152 | bytes 7340032 | tf_op jit(solution)/shard_map/convert_element_type | solution.py:87
  103.5 2.1 convert_element_type.119
  105.6 97.1 %all-to-all-done.2 = bf16[256,4,2048]{2,1,0:T(4,128)(2,1)} async-done(((bf16[256,4,2048]{2,1,0:T(4,128)(2,1)}), bf16[256,4,2048]{2,1,0:T(4,128)(2,1)}, u32[]{:S(2)}, u32[]{:S(2)}) %all-to-all-start.2) | async-done | bytes 4194336 | tf_op jit(solution)/shard_map/all_to_all | solution.py:14
  202.7 6.9 %reshape.195 = bf16[1024,2048]{1,0:T(8,128)(2,1)} reshape(bf16[256,4,2048]{2,1,0:T(4,128)(2,1)} %all-to-all-done.2) | data formatting | bytes 8388608 | tf_op jit(solution)/shard_map/reshape | solution.py:13
  209.6 19.8 %maximum_convert_fusion = bf16[1024,2048]{1,0:T(8,128)(2,1)} fusion(bf16[2048,2048]{1,0:T(8,128)(2,1)} %all-gather.2.cloned.1.call-done, bf16[1024,1024]{1,0:T(8,128)(2,1)S(1)} %copy-done.1, bf16[1024,2048]{1,0:T(8,128)(2,1)} %reshape.195, f32[2048]{0:T(1024)S(1)} %copy-done.11, f32[2048]{0:T(1024)S(1)} %copy-done.12), kind=kOutput, calls=%fused_computation.2 | convolution fusion | flops 12897484800 | bytes 18890752 | tf_op jit(solution)/shard_map/dot_general | solution.py:23
  229.4 3.4 %fusion.5 = bf16[1024,8]{0,1:T(8,128)(2,1)S(1)} fusion(bf16[1024,2048]{1,0:T(8,128)(2,1)} %maximum_convert_fusion, bf16[2048,8]{0,1:T(8,128)(2,1)S(1)} %copy-done.4, f32[8]{0:T(128)S(1)} %copy-done.9), kind=kOutput, calls=%fused_computation.12 | convolution fusion | flops 33570816 | bytes 4243488 | tf_op jit(solution)/shard_map/dot_general | solution.py:29
  233.8 0.7 reduce.12
  235.1 6.0 %all-to-all-start.3 = ((bf16[32,2,128]{2,1,0:T(2,128)(2,1)}), bf16[32,2,128]{2,1,0:T(2,128)(2,1)S(1)}, u32[]{:S(2)}, u32[]{:S(2)}) async-start(bf16[32,2,128]{2,1,0:T(2,128)(2,1)} %reshape.230), calls=%async_computation.3 | async-start | bytes 32768 | tf_op jit(solution)/shard_map/all_to_all | solution.py:89
  241.3 6.8 %all-to-all-done.3 = bf16[32,2,128]{2,1,0:T(2,128)(2,1)S(1)} async-done(((bf16[32,2,128]{2,1,0:T(2,128)(2,1)}), bf16[32,2,128]{2,1,0:T(2,128)(2,1)S(1)}, u32[]{:S(2)}, u32[]{:S(2)}) %all-to-all-start.3) | async-done | bytes 16416 | tf_op jit(solution)/shard_map/all_to_all | solution.py:89
  (69 shorter events, 9.6 us)
Async XLA Ops:
  7.2 87.3 %copy-start = (bf16[256,1024]{1,0:T(8,128)(2,1)S(1)}, bf16[256,1024]{1,0:T(8,128)(2,1)}, u32[]{:S(2)}) copy-start(bf16[256,1024]{1,0:T(8,128)(2,1)} %param.17) | copy-start | bytes 1572868
  7.2 202.4 %all-gather.2.cloned.1.call-start = ((), (), s32[]{:S(2)}) async-start(), calls=%async_computation.4 | async-start | bytes 8421376 | tf_op jit(solution)/shard_map/all_gather | solution.py:25
  12.4 27.1 %all-to-all-start.1 = ((s32[32,1,8]{2,1,0:T(1,128)}), s32[32,1,8]{2,1,0:T(1,128)S(1)}, u32[]{:S(2)}, u32[]{:S(2)}) async-start(s32[32,1,8]{2,1,0:T(1,128)} %bitcast.3), calls=%async_computation.1 | async-start | bytes 32768 | tf_op jit(solution)/shard_map/all_to_all | solution.py:81
  21.0 8.6 %copy-start.8 = (s32[192,4]{0,1:T(4,128)S(1)}, s32[192,4]{0,1:T(4,128)}, u32[]{:S(2)}) copy-start(s32[192,4]{0,1:T(4,128)} %param.25) | copy-start | bytes 9220
  21.0 8.8 %copy-start.3 = (bf16[128,1024]{1,0:T(8,128)(2,1)S(1)}, bf16[128,1024]{1,0:T(8,128)(2,1)}, u32[]{:S(2)}) copy-start(bf16[128,1024]{1,0:T(8,128)(2,1)} %param.16) | copy-start | bytes 786436
  36.8 39.3 %copy-start.5 = (bf16[4,2048]{1,0:T(4,128)(2,1)S(1)}, bf16[4,2048]{1,0:T(4,128)(2,1)}, u32[]{:S(2)}) copy-start(bf16[4,2048]{1,0:T(4,128)(2,1)} %param.18) | copy-start | bytes 49156
  80.2 12.7 %copy-start.6 = (s32[192,1]{0,1:T(1,128)S(1)}, s32[192,1]{0,1:T(1,128)}, u32[]{:S(2)}) copy-start(s32[192,1]{0,1:T(1,128)} %param.26) | copy-start | bytes 2308
  80.3 12.8 %copy-start.7 = (s32[192]{0:T(256)S(1)}, s32[192]{0:T(256)}, u32[]{:S(2)}) copy-start(s32[192]{0:T(256)} %param.24) | copy-start | bytes 2308
  80.3 122.4 %all-to-all-start.2 = ((bf16[256,4,2048]{2,1,0:T(4,128)(2,1)}), bf16[256,4,2048]{2,1,0:T(4,128)(2,1)}, u32[]{:S(2)}, u32[]{:S(2)}) async-start(bf16[256,4,2048]{2,1,0:T(4,128)(2,1)} %stack.2), calls=%async_computation.2 | async-start | bytes 8388608 | tf_op jit(solution)/shard_map/all_to_all | solution.py:14
  105.6 104.0 %copy-start.1 = (bf16[1024,1024]{1,0:T(8,128)(2,1)S(1)}, bf16[1024,1024]{1,0:T(8,128)(2,1)}, u32[]{:S(2)}) copy-start(bf16[1024,1024]{1,0:T(8,128)(2,1)} %convert_element_type.119) | copy-start | bytes 6291460
  105.6 104.0 %copy-start.11 = (f32[2048]{0:T(1024)S(1)}, f32[2048]{0:T(1024)}, u32[]{:S(2)}) copy-start(f32[2048]{0:T(1024)} %param.21) | copy-start | bytes 24580
  105.6 104.0 %copy-start.12 = (f32[2048]{0:T(1024)S(1)}, f32[2048]{0:T(1024)}, u32[]{:S(2)}) copy-start(f32[2048]{0:T(1024)} %param.19) | copy-start | bytes 24580
  209.6 19.8 %copy-start.4 = (bf16[2048,8]{0,1:T(8,128)(2,1)S(1)}, bf16[2048,8]{0,1:T(8,128)(2,1)}, u32[]{:S(2)}) copy-start(bf16[2048,8]{0,1:T(8,128)(2,1)} %param.22) | copy-start | bytes 98308
  209.6 19.8 %copy-start.9 = (f32[8]{0:T(128)S(1)}, f32[8]{0:T(128)}, u32[]{:S(2)}) copy-start(f32[8]{0:T(128)} %param.23) | copy-start | bytes 100
  229.4 19.6 %copy-start.2 = (s32[192,32]{0,1:T(8,128)S(1)}, s32[192,32]{0,1:T(8,128)}, u32[]{:S(2)}) copy-start(s32[192,32]{0,1:T(8,128)} %param.28) | copy-start | bytes 73732
  229.4 19.8 %copy-start.10 = (s32[192]{0:T(256)S(1)}, s32[192]{0:T(256)}, u32[]{:S(2)}) copy-start(s32[192]{0:T(256)} %param.29) | copy-start | bytes 2308
  235.1 12.9 %all-to-all-start.3 = ((bf16[32,2,128]{2,1,0:T(2,128)(2,1)}), bf16[32,2,128]{2,1,0:T(2,128)(2,1)S(1)}, u32[]{:S(2)}, u32[]{:S(2)}) async-start(bf16[32,2,128]{2,1,0:T(2,128)(2,1)} %reshape.230), calls=%async_computation.3 | async-start | bytes 32768 | tf_op jit(solution)/shard_map/all_to_all | solution.py:89
Sparse Core Ops, SparseCore 0:
  11.6 145.7 all-gather.1
